TPU v7x, 512 devices: a whole 4x8x8 slice. The times are simulated.
512 devices in a mesh: row: 64 (over y, z_hi, core), hid: 8 (over z_lo, x).
Axes of the slice: x: 4, y: 8, z: 8 (z_hi: 4, z_lo: 2; z = z_hi * 2 + z_lo), core: 2. Of those that a mesh axis runs over, the one named last changes fastest.
Arguments:
- features: bfloat16 [256, 256, 512], P('row'), may hold values from -6 to 6
- dw_weight: float32 [2, 7, 7, 512], replicated, may hold values from -0.875 to 0.875
- dw_bias: float32 [2, 512], replicated, may hold values from -3 to 3
- ln_gain: float32 [2, 512], replicated, may hold values from 0.1 to 1.9
- ln_bias: float32 [2, 512], replicated, may hold values from -3 to 3
- w_up: bfloat16 [2, 512, 2048], P(None, None, 'hid'), may hold values from -0.25 to 0.25
- b_up: float32 [2, 2048], P(None, 'hid'), may hold values from -3 to 3
- w_down: bfloat16 [2, 2048, 512], P(None, 'hid'), may hold values from -0.125 to 0.125
- b_down: float32 [2, 512], replicated, may hold values from -3 to 3
- layer_scale: float32 [2, 512], replicated, may hold values from 0.2 to 1
Outputs:
- result_map: bfloat16 [256, 256, 512], P('row')
All inputs are finite; a program needn't handle non-finite values.
Results may differ from a plain program's by a relative error of at most 0.018.
Values may be sent and summed in bfloat16 or wider, within the bound.
A program may use at most 64 MiB of HBM per device.

v0:
```python
import jax
import jax.numpy as jnp
from jax import lax
from jax.sharding import PartitionSpec as P


def extended(block, sides, width):
    for axis, dim in sides:
        count = lax.axis_size(axis)
        forward = [(i, i + 1) for i in range(count - 1)]
        backward = [(target, source) for source, target in forward]
        low = lax.ppermute(
            lax.slice_in_dim(block, block.shape[dim] - width, None, axis=dim), axis, forward
        )
        high = lax.ppermute(lax.slice_in_dim(block, 0, width, axis=dim), axis, backward)
        block = jnp.concatenate([low, block, high], axis=dim)
    return block


def depthwise(padded, kernel, bias):
    pad = kernel.shape[0] // 2
    rows = padded.shape[0] - 2 * pad
    width = padded.shape[1]
    wide = jnp.pad(padded, ((0, 0), (pad, pad), (0, 0)))
    total = jnp.zeros((rows, width, padded.shape[2]), jnp.float32)
    for i in range(kernel.shape[0]):
        for j in range(kernel.shape[1]):
            total = total + wide[i : i + rows, j : j + width, :].astype(jnp.float32) * kernel[i, j]
    return (total + bias).astype(jnp.bfloat16)


def expand(conv, gain, shift, w_first, b_first):
    values = conv.reshape(-1, conv.shape[2]).astype(jnp.float32)
    mean = jnp.mean(values, axis=1, keepdims=True)
    var = jnp.mean((values - mean) ** 2, axis=1, keepdims=True)
    normed = ((values - mean) / jnp.sqrt(var + 1e-06) * gain + shift).astype(jnp.bfloat16)
    return jax.nn.gelu(
        jnp.dot(normed, w_first, preferred_element_type=jnp.float32) + b_first, approximate=False
    ).astype(jnp.bfloat16)


def pointwise(conv, gain, shift, w_first, b_first, w_second):
    hidden = expand(conv, gain, shift, w_first, b_first)
    partial_sum = jnp.dot(hidden, w_second, preferred_element_type=jnp.float32)
    return partial_sum.reshape(conv.shape[0], conv.shape[1], -1)


def shards(features, dw_weight, dw_bias, ln_gain, ln_bias, w_up, b_up, w_down, b_down, layer_scale):
    reach = dw_weight.shape[1] // 2
    state = features
    for b in range(dw_weight.shape[0]):
        padded = extended(state, (("row", 0),), reach)
        conv = depthwise(padded, dw_weight[b], dw_bias[b])
        partial_sum = pointwise(conv, ln_gain[b], ln_bias[b], w_up[b], b_up[b], w_down[b])
        summed = lax.psum(partial_sum.astype(jnp.bfloat16), "hid").astype(jnp.float32)
        state = (state.astype(jnp.float32) + layer_scale[b] * (summed + b_down[b])).astype(
            jnp.bfloat16
        )
    return state


def solution(mesh):
    return jax.shard_map(
        shards,
        mesh=mesh,
        in_specs=(
            P("row", None, None),
            P(),
            P(),
            P(),
            P(),
            P(None, None, "hid"),
            P(None, "hid"),
            P(None, "hid", None),
            P(),
            P(),
        ),
        out_specs=P("row", None, None),
        check_vma=False,
    )
```

profile of v0, /device:TPU:8, one launch (start us, length us, event | category | flops | bytes accessed | tf_op | source)
XLA Modules:
  0.0 297.0 jit_solution(8753654461528168947)
XLA Ops:
  6.5 0.0 all-reduce.5.cloned.1.call-start
  6.6 1.6 fusion.99
  8.2 2.1 collective-permute-start
  10.2 10.3 %collective-permute-start.1 = (bf16[3,256,512]{2,1,0:T(8,128)(2,1)S(1)}, bf16[3,256,512]{2,1,0:T(8,128)(2,1)S(1)}, u32[]{:S(2)}, u32[]{:S(2)}) collective-permute-start(bf16[3,256,512]{2,1,0:T(8,128)(2,1)S(1)} %get-tuple-element.14), channel_id=1, source_target_pairs={{8,0},{16,8},{24,16},{32,24},{40,32},{48,40},{56,48},{64,56},{72,6... | collective-permute-start | bytes 2359304 | tf_op jit(solution)/shard_map/ppermute | solution.py:15
  20.5 0.2 fusion.100
  20.9 14.3 %collective-permute-done = bf16[3,256,512]{2,1,0:T(8,128)(2,1)S(1)} collective-permute-done((bf16[3,256,512]{2,1,0:T(8,128)(2,1)S(1)}, bf16[3,256,512]{2,1,0:T(8,128)(2,1)S(1)}, u32[]{:S(2)}, u32[]{:S(2)}) %collective-permute-start) | collective-permute-done | bytes 786464 | tf_op jit(solution)/shard_map/ppermute | solution.py:12
  35.2 0.1 constant_dynamic-update-slice_fusion.1
  35.3 0.2 constant_dynamic-update-slice_fusion
  35.4 1.9 collective-permute-done.1
  37.3 0.8 select_maximum_fusion.2
  38.2 0.1 constant_dynamic-update-slice_fusion.2
  38.2 16.1 %convert_reduce_fusion.1 = (f32[4,256]{1,0:T(4,128)S(1)}, bf16[4,256,512]{2,1,0:T(8,128)(2,1)S(1)}) fusion(f32[512]{0:T(512)S(1)} %bitcast.241, f32[512]{0:T(512)S(1)} %bitcast.171, bf16[10,262,512]{2,1,0:T(8,128)(2,1)S(1)} %select_maximum_fusion.2, f32[512]{0:T(512)S(1)} %bitcast.172, f32[512]{0:T(512)S(1)} %bitcast.173, f32[512]{0:T(512)S(1)} %bitcast.174, ...), kind=kLoop, calls=%fused_computation.13 | loop fusion | flops 78642176 | bytes 52535296 | tf_op jit(solution)/shard_map/reduce_sum | solution.py:34
  54.4 0.5 fusion.10
  54.9 0.5 fusion.13
  55.4 2.7 fusion.68
  58.1 1.4 convolution_convert_fusion.1
  59.6 0.0 all-reduce.7.cloned.1.call-start
  59.7 90.2 %all-reduce.5.cloned.1.call-done = bf16[4,256,512]{2,1,0:T(8,128)(2,1)} async-done(((bf16[4,256,512]{2,1,0:T(8,128)(2,1)}), bf16[4,256,512]{2,1,0:T(8,128)(2,1)}) %all-reduce.5.cloned.1.call-update) | async-done | bytes 1048592 | tf_op jit(solution)/shard_map/psum | solution.py:55
  149.9 1.6 fusion.39
  151.5 0.1 fusion.98
  151.6 1.9 collective-permute-start.2
  153.6 6.8 %collective-permute-start.3 = (bf16[3,256,512]{2,1,0:T(8,128)(2,1)S(1)}, bf16[3,256,512]{2,1,0:T(8,128)(2,1)S(1)}, u32[]{:S(2)}, u32[]{:S(2)}) collective-permute-start(bf16[3,256,512]{2,1,0:T(8,128)(2,1)S(1)} %get-tuple-element.10), channel_id=1, source_target_pairs={{8,0},{16,8},{24,16},{32,24},{40,32},{48,40},{56,48},{64,56},{72,6... | collective-permute-start | bytes 2359304 | tf_op jit(solution)/shard_map/ppermute | solution.py:15
  160.5 14.7 %collective-permute-done.2 = bf16[3,256,512]{2,1,0:T(8,128)(2,1)S(1)} collective-permute-done((bf16[3,256,512]{2,1,0:T(8,128)(2,1)S(1)}, bf16[3,256,512]{2,1,0:T(8,128)(2,1)S(1)}, u32[]{:S(2)}, u32[]{:S(2)}) %collective-permute-start.2) | collective-permute-done | bytes 786464 | tf_op jit(solution)/shard_map/ppermute | solution.py:12
  175.2 2.7 collective-permute-done.3
  177.9 0.8 select_maximum_fusion
  178.8 16.3 %convert_reduce_fusion = (f32[4,256]{1,0:T(4,128)S(1)}, bf16[4,256,512]{2,1,0:T(8,128)(2,1)S(1)}) fusion(f32[512]{0:T(512)S(1)} %bitcast.238, f32[512]{0:T(512)S(1)} %bitcast.201, bf16[10,262,512]{2,1,0:T(8,128)(2,1)S(1)} %select_maximum_fusion, f32[512]{0:T(512)S(1)} %bitcast.202, f32[512]{0:T(512)S(1)} %bitcast.203, f32[512]{0:T(512)S(1)} %bitcast.204, ...), kind=kLoop, calls=%fused_computation.9 | loop fusion | flops 81787904 | bytes 47816704 | tf_op jit(solution)/shard_map/reduce_sum | solution.py:34
  195.0 0.5 fusion.6
  195.6 0.5 fusion.9
  196.0 2.7 fusion.71
  198.8 1.4 convolution_convert_fusion
  200.2 87.4 %all-reduce.7.cloned.1.call-done = bf16[4,256,512]{2,1,0:T(8,128)(2,1)} async-done(((bf16[4,256,512]{2,1,0:T(8,128)(2,1)}), bf16[4,256,512]{2,1,0:T(8,128)(2,1)}) %all-reduce.7.cloned.1.call-update) | async-done | bytes 1048592 | tf_op jit(solution)/shard_map/psum | solution.py:55
  287.6 2.6 fusion.65
  (39 shorter events, 0.4 us)
Async XLA Ops:
  6.5 14.0 %copy-start.2 = (f32[2,7,7,512]{3,0,2,1:T(2,128)S(1)}, f32[2,7,7,512]{3,0,2,1:T(2,128)}, u32[]{:S(2)}) copy-start(f32[2,7,7,512]{3,0,2,1:T(2,128)} %param.11) | copy-start | bytes 602116
  6.5 14.2 %copy-start.3 = (f32[2,512]{1,0:T(2,128)S(1)}, f32[2,512]{1,0:T(2,128)}, u32[]{:S(2)}) copy-start(f32[2,512]{1,0:T(2,128)} %param.12) | copy-start | bytes 12292
  6.5 14.2 %copy-start.4 = (f32[2,512]{1,0:T(2,128)S(1)}, f32[2,512]{1,0:T(2,128)}, u32[]{:S(2)}) copy-start(f32[2,512]{1,0:T(2,128)} %param.13) | copy-start | bytes 12292
  6.5 14.3 %copy-start.5 = (f32[2,512]{1,0:T(2,128)S(1)}, f32[2,512]{1,0:T(2,128)}, u32[]{:S(2)}) copy-start(f32[2,512]{1,0:T(2,128)} %param.14) | copy-start | bytes 12292
  6.5 14.3 %copy-start.8 = (f32[2,256]{1,0:T(2,128)S(1)}, f32[2,256]{1,0:T(2,128)}, u32[]{:S(2)}) copy-start(f32[2,256]{1,0:T(2,128)} %param.16) | copy-start | bytes 6148
  6.5 143.3 %all-reduce.5.cloned.1.call-start = ((), (), s32[]{:S(2)}) async-start(), calls=%async_computation | async-start | bytes 2097152 | tf_op jit(solution)/shard_map/psum | solution.py:55
  8.2 27.1 %copy-start = (bf16[4,256,512]{2,1,0:T(8,128)(2,1)S(1)}, bf16[4,256,512]{2,1,0:T(8,128)(2,1)}, u32[]{:S(2)}) copy-start(bf16[4,256,512]{2,1,0:T(8,128)(2,1)} %param.10) | copy-start | bytes 3145732
  8.2 27.0 %collective-permute-start = (bf16[3,256,512]{2,1,0:T(8,128)(2,1)S(1)}, bf16[3,256,512]{2,1,0:T(8,128)(2,1)S(1)}, u32[]{:S(2)}, u32[]{:S(2)}) collective-permute-start(bf16[3,256,512]{2,1,0:T(8,128)(2,1)S(1)} %get-tuple-element.13), channel_id=1, source_target_pairs={{0,8},{8,16},{16,24},{24,32},{32,40},{40,48},{48,56},{56,64},{64,7... | collective-permute-start | bytes 2359304 | tf_op jit(solution)/shard_map/ppermute | solution.py:12
  10.2 27.1 %collective-permute-start.1 = (bf16[3,256,512]{2,1,0:T(8,128)(2,1)S(1)}, bf16[3,256,512]{2,1,0:T(8,128)(2,1)S(1)}, u32[]{:S(2)}, u32[]{:S(2)}) collective-permute-start(bf16[3,256,512]{2,1,0:T(8,128)(2,1)S(1)} %get-tuple-element.14), channel_id=1, source_target_pairs={{8,0},{16,8},{24,16},{32,24},{40,32},{48,40},{56,48},{64,56},{72,6... | collective-permute-start | bytes 2359304 | tf_op jit(solution)/shard_map/ppermute | solution.py:15
  54.3 1.0 copy-start.9
  55.4 2.8 copy-start.1
  58.1 1.5 copy-start.6
  58.1 1.5 copy-start.7
  59.6 228.0 %all-reduce.7.cloned.1.call-start = ((), (), s32[]{:S(2)}) async-start(), calls=%async_computation.1 | async-start | bytes 2097152 | tf_op jit(solution)/shard_map/psum | solution.py:55
  151.6 23.6 %collective-permute-start.2 = (bf16[3,256,512]{2,1,0:T(8,128)(2,1)S(1)}, bf16[3,256,512]{2,1,0:T(8,128)(2,1)S(1)}, u32[]{:S(2)}, u32[]{:S(2)}) collective-permute-start(bf16[3,256,512]{2,1,0:T(8,128)(2,1)S(1)} %get-tuple-element.9), channel_id=1, source_target_pairs={{0,8},{8,16},{16,24},{24,32},{32,40},{40,48},{48,56},{56,64},{64,7... | collective-permute-start | bytes 2359304 | tf_op jit(solution)/shard_map/ppermute | solution.py:12
  153.6 24.3 %collective-permute-start.3 = (bf16[3,256,512]{2,1,0:T(8,128)(2,1)S(1)}, bf16[3,256,512]{2,1,0:T(8,128)(2,1)S(1)}, u32[]{:S(2)}, u32[]{:S(2)}) collective-permute-start(bf16[3,256,512]{2,1,0:T(8,128)(2,1)S(1)} %get-tuple-element.10), channel_id=1, source_target_pairs={{8,0},{16,8},{24,16},{32,24},{40,32},{48,40},{56,48},{64,56},{72,6... | collective-permute-start | bytes 2359304 | tf_op jit(solution)/shard_map/ppermute | solution.py:15
Sparse Core Ops, SparseCore 0:
  59.7 90.1 all-reduce.4
  200.3 87.2 all-reduce.6
where the time goes:
time: 297 us
  waiting for transfers between devices  211 us (71%)
  other arithmetic  40.2 us (14%)
  starting transfers between devices  21.1 us (7%)
  between operations  13.8 us (5%)
  matrix products  8.25 us (3%)
    psum x2, waiting for transfers between devices, shards(): lax.psum(partial_sum.astype(jnp.bfloat16), 'hid').astype(jnp.float32)  178 us
    reduce_sum x2, other arithmetic, expand(): mean = jnp.mean(values, axis=1, keepdims=True)  32.3 us
    ppermute x2, waiting for transfers between devices, extended(): lax.ppermute(lax.slice_in_dim(block, block.shape[dim] - width, None, axis...  29 us
    ppermute x2, starting transfers between devices, extended(): lax.ppermute(lax.slice_in_dim(block, 0, width, axis=dim), axis, backward)  17.1 us
  transfers between devices with their start and end apart: 6, of which 6 were waited for; matrix products, arithmetic and copies ran while one was open for 0% of the time, Pallas kernels for 0%

commit v1 on v0

--- a/solution.py
+++ b/solution.py
@@ -52,7 +52,9 @@
         padded = extended(state, (("row", 0),), reach)
         conv = depthwise(padded, dw_weight[b], dw_bias[b])
         partial_sum = pointwise(conv, ln_gain[b], ln_bias[b], w_up[b], b_up[b], w_down[b])
-        summed = lax.psum(partial_sum.astype(jnp.bfloat16), "hid").astype(jnp.float32)
+        summed = jnp.sum(lax.all_gather(partial_sum.astype(jnp.bfloat16), "hid"), axis=0).astype(
+            jnp.float32
+        )
         state = (state.astype(jnp.float32) + layer_scale[b] * (summed + b_down[b])).astype(
             jnp.bfloat16
         )

time: 297 us -> 324 us (1.091)
  the two profiles are of different devices: /device:TPU:8 before, /device:TPU:1 now
where the time goes in v1:
time: 324 us; the launch traced here: 323 us
  waiting for transfers between devices  234 us (72%)
  other arithmetic  47.3 us (15%)
  starting transfers between devices  17.4 us (5%)
  between operations  13.8 us (4%)
  matrix products  8.25 us (3%)
    all_gather x2, waiting for transfers between devices, shards(): lax.all_gather(partial_sum.astype(jnp.bfloat16), 'hid')  190 us
    reduce_sum x2, other arithmetic, expand(): mean = jnp.mean(values, axis=1, keepdims=True)  32.3 us
    ppermute x2, waiting for transfers between devices, extended(): lax.ppermute(lax.slice_in_dim(block, 0, width, axis=dim), axis, backward)  31.5 us
    ppermute x2, waiting for transfers between devices, extended(): lax.ppermute(lax.slice_in_dim(block, block.shape[dim] - width, None, axis...  12.3 us
    ppermute x2, starting transfers between devices, extended(): lax.ppermute(lax.slice_in_dim(block, block.shape[dim] - width, None, axis...  12.2 us
    reduce_sum x2, other arithmetic, shards(): jnp.sum(lax.all_gather(partial_sum.astype(jnp.bfloat16), 'hid'), axis=0)  9.51 us
  transfers between devices with their start and end apart: 6, of which 6 were waited for; matrix products, arithmetic and copies ran while one was open for 0% of the time, Pallas kernels for 0%

profile of v1, /device:TPU:1, one launch (start us, length us, event | category | flops | bytes accessed | tf_op | source)
XLA Modules:
  0.0 323.2 jit_solution(16281486637602460793)
XLA Ops:
  6.6 1.6 fusion.99
  8.2 7.3 %collective-permute-start = (bf16[3,256,512]{2,1,0:T(8,128)(2,1)S(1)}, bf16[3,256,512]{2,1,0:T(8,128)(2,1)S(1)}, u32[]{:S(2)}, u32[]{:S(2)}) collective-permute-start(bf16[3,256,512]{2,1,0:T(8,128)(2,1)S(1)} %get-tuple-element.13), channel_id=1, source_target_pairs={{0,8},{8,16},{16,24},{24,32},{32,40},{40,48},{48,56},{56,64},{64,7... | collective-permute-start | bytes 2359304 | tf_op jit(solution)/shard_map/ppermute | solution.py:12
  15.5 2.9 collective-permute-start.1
  18.5 0.2 fusion.100
  18.9 5.6 %collective-permute-done = bf16[3,256,512]{2,1,0:T(8,128)(2,1)S(1)} collective-permute-done((bf16[3,256,512]{2,1,0:T(8,128)(2,1)S(1)}, bf16[3,256,512]{2,1,0:T(8,128)(2,1)S(1)}, u32[]{:S(2)}, u32[]{:S(2)}) %collective-permute-start) | collective-permute-done | bytes 786464 | tf_op jit(solution)/shard_map/ppermute | solution.py:12
  24.5 0.1 constant_dynamic-update-slice_fusion.1
  24.5 0.2 constant_dynamic-update-slice_fusion
  24.7 16.1 %collective-permute-done.1 = bf16[3,256,512]{2,1,0:T(8,128)(2,1)S(1)} collective-permute-done((bf16[3,256,512]{2,1,0:T(8,128)(2,1)S(1)}, bf16[3,256,512]{2,1,0:T(8,128)(2,1)S(1)}, u32[]{:S(2)}, u32[]{:S(2)}) %collective-permute-start.1) | collective-permute-done | bytes 786464 | tf_op jit(solution)/shard_map/ppermute | solution.py:15
  40.8 0.8 select_maximum_fusion.2
  41.7 0.1 constant_dynamic-update-slice_fusion.2
  41.8 16.1 %convert_reduce_fusion.1 = (f32[4,256]{1,0:T(4,128)S(1)}, bf16[4,256,512]{2,1,0:T(8,128)(2,1)S(1)}) fusion(f32[512]{0:T(512)S(1)} %bitcast.245, f32[512]{0:T(512)S(1)} %bitcast.175, bf16[10,262,512]{2,1,0:T(8,128)(2,1)S(1)} %select_maximum_fusion.2, f32[512]{0:T(512)S(1)} %bitcast.176, f32[512]{0:T(512)S(1)} %bitcast.177, f32[512]{0:T(512)S(1)} %bitcast.178, ...), kind=kLoop, calls=%fused_computation.13 | loop fusion | flops 78642176 | bytes 52535296 | tf_op jit(solution)/shard_map/reduce_sum | solution.py:34
  57.9 0.5 fusion.10
  58.4 0.5 fusion.13
  58.9 2.7 fusion.68
  61.7 1.4 convolution_convert_fusion.1
  63.2 97.1 %all-gather.5.cloned.1.call-done = bf16[32,256,512]{2,1,0:T(8,128)(2,1)} async-done(((bf16[4,256,512]{2,1,0:T(8,128)(2,1)}), bf16[32,256,512]{2,1,0:T(8,128)(2,1)}) %all-gather.5.cloned.1.call-update) | async-done | bytes 8388624 | tf_op jit(solution)/shard_map/all_gather | solution.py:55
  160.3 4.8 %reduce_sum.62 = bf16[4,256,512]{2,1,0:T(8,128)(2,1)S(1)} reduce(bf16[8,4,256,512]{3,2,1,0:T(8,128)(2,1)} %bitcast.138, bf16[]{:T(256)} %constant.33.clone.1), dimensions={0}, to_apply=%region_2.3 | reduce | flops 3670016 | bytes 9437186 | tf_op jit(solution)/shard_map/reduce_sum | solution.py:55
  165.0 0.4 fusion.39
  165.4 0.1 fusion.98
  165.6 4.9 %collective-permute-start.2 = (bf16[3,256,512]{2,1,0:T(8,128)(2,1)S(1)}, bf16[3,256,512]{2,1,0:T(8,128)(2,1)S(1)}, u32[]{:S(2)}, u32[]{:S(2)}) collective-permute-start(bf16[3,256,512]{2,1,0:T(8,128)(2,1)S(1)} %get-tuple-element.9), channel_id=1, source_target_pairs={{0,8},{8,16},{16,24},{24,32},{32,40},{40,48},{48,56},{56,64},{64,7... | collective-permute-start | bytes 2359304 | tf_op jit(solution)/shard_map/ppermute | solution.py:12
  170.5 2.1 collective-permute-start.3
  172.7 6.7 %collective-permute-done.2 = bf16[3,256,512]{2,1,0:T(8,128)(2,1)S(1)} collective-permute-done((bf16[3,256,512]{2,1,0:T(8,128)(2,1)S(1)}, bf16[3,256,512]{2,1,0:T(8,128)(2,1)S(1)}, u32[]{:S(2)}, u32[]{:S(2)}) %collective-permute-start.2) | collective-permute-done | bytes 786464 | tf_op jit(solution)/shard_map/ppermute | solution.py:12
  179.4 15.4 %collective-permute-done.3 = bf16[3,256,512]{2,1,0:T(8,128)(2,1)S(1)} collective-permute-done((bf16[3,256,512]{2,1,0:T(8,128)(2,1)S(1)}, bf16[3,256,512]{2,1,0:T(8,128)(2,1)S(1)}, u32[]{:S(2)}, u32[]{:S(2)}) %collective-permute-start.3) | collective-permute-done | bytes 786464 | tf_op jit(solution)/shard_map/ppermute | solution.py:15
  194.8 0.8 select_maximum_fusion
  195.7 16.3 %convert_reduce_fusion = (f32[4,256]{1,0:T(4,128)S(1)}, bf16[4,256,512]{2,1,0:T(8,128)(2,1)S(1)}) fusion(f32[512]{0:T(512)S(1)} %bitcast.242, f32[512]{0:T(512)S(1)} %bitcast.224, bf16[10,262,512]{2,1,0:T(8,128)(2,1)S(1)} %select_maximum_fusion, f32[512]{0:T(512)S(1)} %bitcast.225, f32[512]{0:T(512)S(1)} %bitcast.226, f32[512]{0:T(512)S(1)} %bitcast.227, ...), kind=kLoop, calls=%fused_computation.9 | loop fusion | flops 81787904 | bytes 47816704 | tf_op jit(solution)/shard_map/reduce_sum | solution.py:34
  212.0 0.5 fusion.6
  212.5 0.5 fusion.9
  213.0 2.7 fusion.71
  215.8 1.4 convolution_convert_fusion
  217.2 93.0 %all-gather.7.cloned.1.call-done = bf16[32,256,512]{2,1,0:T(8,128)(2,1)} async-done(((bf16[4,256,512]{2,1,0:T(8,128)(2,1)}), bf16[32,256,512]{2,1,0:T(8,128)(2,1)}) %all-gather.7.cloned.1.call-update) | async-done | bytes 8388624 | tf_op jit(solution)/shard_map/all_gather | solution.py:55
  310.2 4.8 %reduce_sum.65 = bf16[4,256,512]{2,1,0:T(8,128)(2,1)S(1)} reduce(bf16[8,4,256,512]{3,2,1,0:T(8,128)(2,1)} %bitcast.139, bf16[]{:T(256)} %constant.33.clone.1), dimensions={0}, to_apply=%region_5.6 | reduce | flops 3670016 | bytes 9437186 | tf_op jit(solution)/shard_map/reduce_sum | solution.py:55
  315.0 1.4 fusion.65
  (45 shorter events, 0.5 us)
Async XLA Ops:
  6.5 11.9 %copy-start.4 = (f32[2,512]{1,0:T(2,128)S(1)}, f32[2,512]{1,0:T(2,128)}, u32[]{:S(2)}) copy-start(f32[2,512]{1,0:T(2,128)} %param.12) | copy-start | bytes 12292
  6.5 11.9 %copy-start.5 = (f32[2,512]{1,0:T(2,128)S(1)}, f32[2,512]{1,0:T(2,128)}, u32[]{:S(2)}) copy-start(f32[2,512]{1,0:T(2,128)} %param.13) | copy-start | bytes 12292
  6.5 12.0 %copy-start.3 = (f32[2,7,7,512]{3,0,2,1:T(2,128)S(1)}, f32[2,7,7,512]{3,0,2,1:T(2,128)}, u32[]{:S(2)}) copy-start(f32[2,7,7,512]{3,0,2,1:T(2,128)} %param.11) | copy-start | bytes 602116
  6.5 12.2 %copy-start.6 = (f32[2,512]{1,0:T(2,128)S(1)}, f32[2,512]{1,0:T(2,128)}, u32[]{:S(2)}) copy-start(f32[2,512]{1,0:T(2,128)} %param.14) | copy-start | bytes 12292
  6.5 12.2 %copy-start.9 = (f32[2,256]{1,0:T(2,128)S(1)}, f32[2,256]{1,0:T(2,128)}, u32[]{:S(2)}) copy-start(f32[2,256]{1,0:T(2,128)} %param.16) | copy-start | bytes 6148
  6.5 153.7 %all-gather.5.cloned.1.call-start = ((), (), s32[]{:S(2)}) async-start(), calls=%async_computation | async-start | bytes 9437184 | tf_op jit(solution)/shard_map/all_gather | solution.py:55
  8.2 16.4 %copy-start = (bf16[4,256,512]{2,1,0:T(8,128)(2,1)S(1)}, bf16[4,256,512]{2,1,0:T(8,128)(2,1)}, u32[]{:S(2)}) copy-start(bf16[4,256,512]{2,1,0:T(8,128)(2,1)} %param.10) | copy-start | bytes 3145732
  8.2 16.3 %collective-permute-start = (bf16[3,256,512]{2,1,0:T(8,128)(2,1)S(1)}, bf16[3,256,512]{2,1,0:T(8,128)(2,1)S(1)}, u32[]{:S(2)}, u32[]{:S(2)}) collective-permute-start(bf16[3,256,512]{2,1,0:T(8,128)(2,1)S(1)} %get-tuple-element.13), channel_id=1, source_target_pairs={{0,8},{8,16},{16,24},{24,32},{32,40},{40,48},{48,56},{56,64},{64,7... | collective-permute-start | bytes 2359304 | tf_op jit(solution)/shard_map/ppermute | solution.py:12
  15.5 25.3 %collective-permute-start.1 = (bf16[3,256,512]{2,1,0:T(8,128)(2,1)S(1)}, bf16[3,256,512]{2,1,0:T(8,128)(2,1)S(1)}, u32[]{:S(2)}, u32[]{:S(2)}) collective-permute-start(bf16[3,256,512]{2,1,0:T(8,128)(2,1)S(1)} %get-tuple-element.14), channel_id=1, source_target_pairs={{8,0},{16,8},{24,16},{32,24},{40,32},{48,40},{56,48},{64,56},{72,6... | collective-permute-start | bytes 2359304 | tf_op jit(solution)/shard_map/ppermute | solution.py:15
  57.8 1.0 copy-start.10
  58.9 2.8 copy-start.1
  61.6 1.5 copy-start.7
  61.6 1.5 copy-start.8
  63.1 247.1 %all-gather.7.cloned.1.call-start = ((), (), s32[]{:S(2)}) async-start(), calls=%async_computation.1 | async-start | bytes 9437184 | tf_op jit(solution)/shard_map/all_gather | solution.py:55
  165.6 13.9 %collective-permute-start.2 = (bf16[3,256,512]{2,1,0:T(8,128)(2,1)S(1)}, bf16[3,256,512]{2,1,0:T(8,128)(2,1)S(1)}, u32[]{:S(2)}, u32[]{:S(2)}) collective-permute-start(bf16[3,256,512]{2,1,0:T(8,128)(2,1)S(1)} %get-tuple-element.9), channel_id=1, source_target_pairs={{0,8},{8,16},{16,24},{24,32},{32,40},{40,48},{48,56},{56,64},{64,7... | collective-permute-start | bytes 2359304 | tf_op jit(solution)/shard_map/ppermute | solution.py:12
  170.5 24.4 %collective-permute-start.3 = (bf16[3,256,512]{2,1,0:T(8,128)(2,1)S(1)}, bf16[3,256,512]{2,1,0:T(8,128)(2,1)S(1)}, u32[]{:S(2)}, u32[]{:S(2)}) collective-permute-start(bf16[3,256,512]{2,1,0:T(8,128)(2,1)S(1)} %get-tuple-element.10), channel_id=1, source_target_pairs={{8,0},{16,8},{24,16},{32,24},{40,32},{48,40},{56,48},{64,56},{72,6... | collective-permute-start | bytes 2359304 | tf_op jit(solution)/shard_map/ppermute | solution.py:15
  212.0 1.0 copy-start.11
  213.0 2.7 copy-start.2
Sparse Core Ops, SparseCore 0:
  63.2 96.9 all-gather.4
  217.3 92.8 all-gather.6
